TPU v7x, 512 devices: a whole 4x4x16 slice. The times are simulated.
512 devices in a mesh: chan: 32 (over y, z_lo, core), freq: 16 (over z_hi, x).
Axes of the slice: x: 4, y: 4, z: 16 (z_hi: 4, z_lo: 4; z = z_hi * 4 + z_lo), core: 2. Of those that a mesh axis runs over, the one named last changes fastest.
Arguments:
- spectra: bfloat16 [2, 30, 1024, 4096], P(None, None, 'freq', 'chan'), may hold values from -6 to 6
- src_ids: int32 [2, 32], replicated, may hold values from 0 to 4095
- pair_bin: int32 [2, 32, 4096], P(None, None, 'chan'), may hold values from 0 to 1023, as said below
- slot_of_bin: int32 [1024], replicated, may hold values from 0 to 1023, each once
Outputs:
- offset_gather: float32 [1024, 256], P('chan')
Inputs may be any that keep to these rules, and one draw needn't show every extreme that they name: slot_of_bin names every row of offset_gather once. `pair_bin`: some offset bins are named by no pair.
All inputs are finite; a program needn't handle non-finite values.
Results may differ from a plain program's by a relative error of at most 0.0003.
Values may be sent and summed in bfloat16 or wider, within the bound.
A program may use at most 64 MiB of HBM per device.

v0:
```python
import math
import jax
import jax.numpy as jnp
from jax import lax
from jax.sharding import PartitionSpec as P

F = 1024
NLAG = 256


def lag_basis(anchor, amount, totals, lag_count, windows):
    frequency = anchor + lax.iota(jnp.int32, amount)
    shifts = lax.iota(jnp.int32, lag_count) - lag_count // 2
    phases = frequency[:, None] * shifts[None, :] % (2 * totals)
    angles = phases.astype(jnp.float32) * (math.pi / totals)
    factor = 1.0 / math.sqrt(windows * totals)
    return jnp.concatenate([jnp.cos(angles), -jnp.sin(angles)], axis=0) * factor


def picked(spectra, wanted):
    chans = spectra.shape[3]
    chan_ids = lax.axis_index("chan") * chans + lax.iota(jnp.int32, chans)
    picker = (chan_ids[:, None] == wanted[None, :]).astype(spectra.dtype)
    return jnp.einsum("kwfc,cs->kwfs", spectra, picker, preferred_element_type=jnp.float32)


def cross_terms(source, spectra):
    flipped = jnp.stack([-source[1], source[0]])
    stacked = jnp.stack([source, flipped])
    crossed = jnp.einsum("jkwfs,kwfc->scjf", stacked, spectra, preferred_element_type=jnp.float32)
    return crossed.reshape(source.shape[3] * spectra.shape[3], 2 * spectra.shape[2])


def body(spectra, src_ids, pair_bin, slot_of_bin):
    windows = spectra.shape[1]
    freq_dev = spectra.shape[2]
    steps = pair_bin.shape[0]
    bin_total = slot_of_bin.shape[0]
    lag_table = lag_basis(lax.axis_index("freq") * freq_dev, freq_dev, F, NLAG, windows)
    counts = jnp.zeros((bin_total,), jnp.float32)
    summed = jnp.zeros((bin_total, NLAG), jnp.float32)
    for step_no in range(steps):
        source = lax.psum(picked(spectra, src_ids[step_no]).astype(jnp.bfloat16), "chan")
        crossed = cross_terms(source, spectra)
        bin_ids = pair_bin[step_no].reshape(-1)
        counts = counts + jax.ops.segment_sum(
            jnp.ones((bin_ids.shape[0],), jnp.float32), bin_ids, num_segments=bin_total
        )
        traces = jnp.dot(crossed, lag_table, precision=lax.Precision.HIGHEST)
        summed = summed + jax.ops.segment_sum(traces, bin_ids, num_segments=bin_total)
    summed = jax.ops.segment_sum(summed, slot_of_bin, num_segments=bin_total)
    counts = jax.ops.segment_sum(counts, slot_of_bin, num_segments=bin_total)
    owned, owned_counts = (
        lax.psum_scatter(summed, "chan", scatter_dimension=0, tiled=True),
        lax.psum_scatter(counts, "chan", scatter_dimension=0, tiled=True),
    )
    totals = lax.psum(owned, "freq")
    return totals / jnp.sqrt(jnp.maximum(owned_counts, 1.0))[:, None]


def solution(mesh):
    return jax.shard_map(
        body,
        mesh=mesh,
        in_specs=(P(None, None, "freq", "chan"), P(), P(None, None, "chan"), P()),
        out_specs=P("chan", None),
        check_vma=False,
    )
```

profile of v0, /device:TPU:128, one launch (start us, length us, event | category | flops | bytes accessed | tf_op | source)
XLA Modules:
  0.0 636.5 jit_solution(4346508088757996681)
XLA Ops:
  6.5 0.8 slice_bitcast_fusion.2
  7.3 0.4 copy-done
  7.8 1.8 fusion.6
  9.6 1.8 fusion.7
  11.5 0.3 fusion.22
  11.9 288.8 %all-reduce.4.cloned.1.call-done = (bf16[2,30,64,32]{2,3,1,0:T(8,128)(2,1)}, bf16[2,30,64,32]{2,3,1,0:T(8,128)(2,1)}) async-done(((bf16[2,30,64,32]{2,3,1,0:T(8,128)(2,1)}, bf16[2,30,64,32]{2,3,1,0:T(8,128)(2,1)}), (bf16[2,30,64,32]{2,3,1,0:T(8,128)(2,1)}, bf16[2,30,64,32]{2,3,1,0:T(8,128)(2,1)})) %all-reduce.4.cloned.1.call-update) | async-done | bytes 491536 | tf_op jit(solution)/shard_map/psum | solution.py:43
  300.6 2.1 slice_negate_fusion
  302.8 0.1 maximum_bitcast_fusion
  302.9 1.2 pad_maximum_fusion
  304.1 4.5 copy.15
  308.6 1.2 convolution_bitcast_fusion.1
  309.7 0.2 copy.17
  309.9 0.7 copy-done.3
  310.7 0.1 maximum_bitcast_fusion.1
  310.8 0.1 copy-done.1
  310.9 1.2 pad_maximum_fusion.1
  312.1 5.3 copy.18
  317.4 2.8 convolution_bitcast_fusion
  320.2 0.2 copy.20
  320.4 6.1 fusion.3
  326.5 6.1 fusion
  332.6 23.3 %scatter_custom_fusion = f32[1024,256]{1,0:T(8,128)S(1)} fusion(s32[4096]{0:T(1024)S(1)} %get-tuple-element.12, f32[4096,256]{1,0:T(8,128)} %fusion.3, f32[]{:T(128)} %constant.13.clone.1), kind=kCustom, calls=%fused_computation.27 | custom fusion | flops 1048576 | bytes 1049088 | tf_op jit(solution)/shard_map/scatter-add | solution.py:50
  355.9 23.1 %scatter_custom_fusion.1 = f32[1024,256]{1,0:T(8,128)S(1)} fusion(s32[4096]{0:T(1024)S(1)} %get-tuple-element.11, f32[4096,256]{1,0:T(8,128)} %fusion, f32[]{:T(128)} %constant.13.clone.1), kind=kCustom, calls=%fused_computation.25 | custom fusion | flops 1048576 | bytes 1049088 | tf_op jit(solution)/shard_map/scatter-add | solution.py:50
  379.0 7.3 %scatter_custom_fusion.2 = f32[1024,256]{1,0:T(8,128)} fusion(s32[1024]{0:T(1024)} %param.7, f32[1024,256]{1,0:T(8,128)S(1)} %scatter_custom_fusion, f32[1024,256]{1,0:T(8,128)S(1)} %scatter_custom_fusion.1, f32[]{:T(128)} %constant.13.clone.1), kind=kCustom, calls=%fused_computation.18 | custom fusion | flops 524288 | bytes 3146240 | tf_op jit(solution)/shard_map/scatter-add | solution.py:51
  386.3 28.8 %scatter_custom_fusion.3 = f32[1024]{0:T(1024)S(1)} fusion(s32[4096]{0:T(1024)S(1)} %get-tuple-element.12, f32[4096]{0:T(1024)S(1)} %broadcast.36, f32[]{:T(128)} %constant.13.clone.1), kind=kCustom, calls=%fused_computation.61 | custom fusion | flops 4096 | bytes 4100 | tf_op jit(solution)/shard_map/scatter-add | solution.py:46
  415.1 28.8 %scatter_custom_fusion.4 = f32[1024]{0:T(1024)S(1)} fusion(s32[4096]{0:T(1024)S(1)} %get-tuple-element.11, f32[4096]{0:T(1024)S(1)} %broadcast.36, f32[]{:T(128)} %constant.13.clone.1), kind=kCustom, calls=%fused_computation.59 | custom fusion | flops 4096 | bytes 4100 | tf_op jit(solution)/shard_map/scatter-add | solution.py:46
  443.9 7.8 %scatter_custom_fusion.5 = f32[1024]{0:T(1024)S(1)} fusion(s32[1024]{0:T(1024)} %param.7, f32[1024]{0:T(1024)S(1)} %add.67, f32[]{:T(128)} %constant.13.clone.1), kind=kCustom, calls=%fused_computation.57 | custom fusion | flops 1024 | bytes 4608 | tf_op jit(solution)/shard_map/scatter-add | solution.py:52
  451.7 1.3 dynamic-slice
  453.6 69.6 %all-reduce = f32[1024]{0:T(1024)S(1)} all-reduce(f32[1024]{0:T(1024)S(1)} %scatter_custom_fusion.5), channel_id=3, replica_groups=mesh['chan'=32,'freq'=16] {'chan'}, use_global_device_ids=true, to_apply=%region_10.11.clone | all-reduce | flops 1024 | bytes 8192
  523.2 12.4 %reduce-scatter.2.cloned.1.call-done = f32[32,256]{1,0:T(8,128)} async-done(((f32[1024,256]{1,0:T(8,128)}), f32[32,256]{1,0:T(8,128)}) %reduce-scatter.2.cloned.1.call-update) | async-done | bytes 32784 | tf_op jit(solution)/shard_map/reduce_scatter | solution.py:54
  535.6 93.4 %psum.23 = f32[32,256]{1,0:T(8,128)S(1)} all-reduce(f32[32,256]{1,0:T(8,128)} %reduce-scatter.2.cloned.1.call-done), channel_id=1, replica_groups=mesh['chan'=32,'freq'=16] {'freq'}, use_global_device_ids=true, to_apply=%region_6.7 | all-reduce | flops 8192 | bytes 65536 | tf_op jit(solution)/shard_map/psum | solution.py:57
  629.0 0.7 broadcast_divide_fusion
  (18 shorter events, 0.2 us)
Async XLA Ops:
  6.5 1.2 copy-start
  6.5 5.0 copy-start.4
  6.5 294.1 %all-reduce.4.cloned.1.call-start = ((), (), s32[]{:S(2)}) async-start(), calls=%async_computation.2 | async-start | bytes 1966080 | tf_op jit(solution)/shard_map/psum | solution.py:43
  11.4 524.2 %reduce-scatter.2.cloned.1.call-start = ((), (), s32[]{:S(2)}) async-start(), calls=%async_computation.1 | async-start | bytes 1081344 | tf_op jit(solution)/shard_map/reduce_scatter | solution.py:54
  300.6 2.3 copy-start.2
  309.7 0.9 copy-start.3
  309.7 1.2 copy-start.1
Sparse Core Ops, SparseCore 0:
  11.6 289.0 all-reduce.3
  386.4 149.1 reduce-scatter.1
where the time goes:
time: 637 us
  waiting for transfers between devices  301 us (47%)
  blocking collectives  163 us (26%)
  other arithmetic  125 us (20%)
  matrix products  19.8 us (3%)
  between operations  14.2 us (2%)
  local copies, waits for them, and re-layouts  13.6 us (2%)
    psum x1, waiting for transfers between devices, body(): lax.psum(picked(spectra, src_ids[step_no]).astype(jnp.bfloat16), 'chan')  289 us
    psum x1, blocking collectives, body(): totals = lax.psum(owned, 'freq')  93.4 us
    unnamed x1, blocking collectives  69.6 us
    scatter-add x2, other arithmetic, body(): jax.ops.segment_sum(jnp.ones((bin_ids.shape[0],), jnp.float32), bin_ids,...  57.6 us
    scatter-add x2, other arithmetic, body(): jax.ops.segment_sum(traces, bin_ids, num_segments=bin_total)  46.4 us
  transfers between devices with their start and end apart: 2, of which 2 were waited for; matrix products, arithmetic and copies ran while one was open for 11% of the time, Pallas kernels for 0%

commit v1 on v0

--- a/solution.py
+++ b/solution.py
@@ -40,7 +40,9 @@
     counts = jnp.zeros((bin_total,), jnp.float32)
     summed = jnp.zeros((bin_total, NLAG), jnp.float32)
     for step_no in range(steps):
-        source = lax.psum(picked(spectra, src_ids[step_no]).astype(jnp.bfloat16), "chan")
+        own = picked(spectra, src_ids[step_no]).astype(jnp.bfloat16)
+        blocks = lax.all_gather(own, "chan")
+        source = jnp.sum(blocks, axis=0)
         crossed = cross_terms(source, spectra)
         bin_ids = pair_bin[step_no].reshape(-1)
         counts = counts + jax.ops.segment_sum(

time: 637 us -> 561 us (0.88)
  waiting for transfers between devices: 301 us -> 206 us
  other arithmetic: 125 us -> 141 us
    psum x1 -> x0, waiting for transfers between devices: 289 us -> none  [body(): lax.psum(picked(spectra, src_ids[step_no]).astype(jnp.bfloat16), 'chan')]
    all_gather x0 -> x2, waiting for transfers between devices: none -> 194 us  [body(): blocks = lax.all_gather(own, 'chan')]
    reduce_sum x0 -> x2, other arithmetic: none -> 17.9 us  [body(): source = jnp.sum(blocks, axis=0)]
  transfers between devices with their start and end apart: 2 -> 3, of which waited for: 2 -> 3; matrix products, arithmetic and copies ran while one was open for 11% -> 14% of each run, Pallas kernels for 0% -> 0%
where the time goes in v1:
time: 561 us; the launch traced here: 560 us
  waiting for transfers between devices  206 us (37%)
  blocking collectives  165 us (29%)
  other arithmetic  141 us (25%)
  matrix products  19.8 us (4%)
  between operations  13.9 us (2%)
  local copies, waits for them, and re-layouts  13.6 us (2%)
    all_gather x2, waiting for transfers between devices, body(): blocks = lax.all_gather(own, 'chan')  194 us
    psum x1, blocking collectives, body(): totals = lax.psum(owned, 'freq')  93.2 us
    unnamed x1, blocking collectives  72.2 us
    scatter-add x2, other arithmetic, body(): jax.ops.segment_sum(jnp.ones((bin_ids.shape[0],), jnp.float32), bin_ids,...  57.8 us
    scatter-add x2, other arithmetic, body(): jax.ops.segment_sum(traces, bin_ids, num_segments=bin_total)  46.2 us
    reduce_sum x2, other arithmetic, body(): source = jnp.sum(blocks, axis=0)  17.9 us
    dot_general x2, matrix products, body(): traces = jnp.dot(crossed, lag_table, precision=lax.Precision.HIGHEST)  12.2 us
    reduce_scatter x1, waiting for transfers between devices, body(): lax.psum_scatter(summed, 'chan', scatter_dimension=0, tiled=True)  11.8 us
  transfers between devices with their start and end apart: 3, of which 3 were waited for; matrix products, arithmetic and copies ran while one was open for 14% of the time, Pallas kernels for 0%

profile of v1, /device:TPU:128, one launch (start us, length us, event | category | flops | bytes accessed | tf_op | source)
XLA Modules:
  0.0 560.2 jit_solution(1521135735779695859)
XLA Ops:
  6.5 0.8 slice_bitcast_fusion.2
  7.3 0.4 copy-done
  7.8 1.8 fusion.7
  9.7 1.8 fusion.6
  11.6 0.3 fusion.22
  12.0 100.4 %all-gather.7.cloned.1.call-done = bf16[64,30,64,32]{2,3,1,0:T(8,128)(2,1)} async-done(((bf16[2,30,64,32]{2,3,1,0:T(8,128)(2,1)}), bf16[64,30,64,32]{2,3,1,0:T(8,128)(2,1)}) %all-gather.7.cloned.1.call-update) | async-done | bytes 7864336 | tf_op jit(solution)/shard_map/all_gather | solution.py:44
  112.4 9.0 %reduce_sum.25 = bf16[2,30,64,32]{2,3,1,0:T(8,128)(2,1)S(1)} reduce(bf16[32,2,30,64,32]{3,4,2,1,0:T(8,128)(2,1)} %bitcast.63, bf16[]{:T(256)} %constant.35.clone.1), dimensions={0}, to_apply=%region_2.3 | reduce | flops 3809280 | bytes 8110082 | tf_op jit(solution)/shard_map/reduce_sum | solution.py:45
  121.3 93.7 %all-gather.5.cloned.1.call-done = bf16[64,30,64,32]{2,3,1,0:T(8,128)(2,1)} async-done(((bf16[2,30,64,32]{2,3,1,0:T(8,128)(2,1)}), bf16[64,30,64,32]{2,3,1,0:T(8,128)(2,1)}) %all-gather.5.cloned.1.call-update) | async-done | bytes 7864336 | tf_op jit(solution)/shard_map/all_gather | solution.py:44
  215.1 9.0 %reduce_sum.24 = bf16[2,30,64,32]{2,3,1,0:T(8,128)(2,1)S(1)} reduce(bf16[32,2,30,64,32]{3,4,2,1,0:T(8,128)(2,1)} %bitcast.64, bf16[]{:T(256)} %constant.35.clone.1), dimensions={0}, to_apply=%region_0.1 | reduce | flops 3809280 | bytes 8110082 | tf_op jit(solution)/shard_map/reduce_sum | solution.py:45
  224.0 0.8 slice_negate_fusion.1
  225.0 1.2 pad_maximum_fusion.1
  226.2 4.5 copy.18
  230.7 1.2 convolution_bitcast_fusion
  231.9 0.2 copy.20
  232.1 0.7 copy-done.3
  233.0 1.2 pad_maximum_fusion
  234.2 5.3 copy.15
  239.5 2.8 convolution_bitcast_fusion.1
  242.3 0.2 copy.17
  242.5 6.1 %fusion.3 = f32[4096,256]{1,0:T(8,128)} fusion(f32[16,8,32,128]{3,2,1,0:T(8,128)S(1)} %bitcast.66, f32[64,256]{1,0:T(8,128)S(1)} %get-tuple-element.12, f32[64,256]{1,0:T(8,128)S(1)} %get-tuple-element.11), kind=kOutput, calls=%fused_computation.9 | convolution fusion | flops 1610678272 | bytes 6422528 | tf_op jit(solution)/shard_map/dot_general | solution.py:51
  248.6 6.1 %fusion = f32[4096,256]{1,0:T(8,128)} fusion(f32[16,8,32,128]{3,2,1,0:T(8,128)S(1)} %bitcast.65, f32[64,256]{1,0:T(8,128)S(1)} %get-tuple-element.12, f32[64,256]{1,0:T(8,128)S(1)} %get-tuple-element.11), kind=kOutput, calls=%fused_computation.6 | convolution fusion | flops 1610678272 | bytes 6422528 | tf_op jit(solution)/shard_map/dot_general | solution.py:51
  254.7 23.1 %scatter_custom_fusion = f32[1024,256]{1,0:T(8,128)S(1)} fusion(s32[4096]{0:T(1024)S(1)} %get-tuple-element.10, f32[4096,256]{1,0:T(8,128)} %fusion.3, f32[]{:T(128)} %constant.14.clone.1), kind=kCustom, calls=%fused_computation.27 | custom fusion | flops 1048576 | bytes 1049088 | tf_op jit(solution)/shard_map/scatter-add | solution.py:52
  277.8 23.1 %scatter_custom_fusion.1 = f32[1024,256]{1,0:T(8,128)S(1)} fusion(s32[4096]{0:T(1024)S(1)} %get-tuple-element.9, f32[4096,256]{1,0:T(8,128)} %fusion, f32[]{:T(128)} %constant.14.clone.1), kind=kCustom, calls=%fused_computation.25 | custom fusion | flops 1048576 | bytes 1049088 | tf_op jit(solution)/shard_map/scatter-add | solution.py:52
  300.9 7.3 %scatter_custom_fusion.2 = f32[1024,256]{1,0:T(8,128)} fusion(s32[1024]{0:T(1024)} %param.7, f32[1024,256]{1,0:T(8,128)S(1)} %scatter_custom_fusion, f32[1024,256]{1,0:T(8,128)S(1)} %scatter_custom_fusion.1, f32[]{:T(128)} %constant.14.clone.1), kind=kCustom, calls=%fused_computation.18 | custom fusion | flops 524288 | bytes 3146240 | tf_op jit(solution)/shard_map/scatter-add | solution.py:53
  308.2 28.8 %scatter_custom_fusion.4 = f32[1024]{0:T(1024)S(1)} fusion(s32[4096]{0:T(1024)S(1)} %get-tuple-element.9, f32[4096]{0:T(1024)S(1)} %broadcast.36, f32[]{:T(128)} %constant.14.clone.1), kind=kCustom, calls=%fused_computation.59 | custom fusion | flops 4096 | bytes 4100 | tf_op jit(solution)/shard_map/scatter-add | solution.py:48
  337.0 29.0 %scatter_custom_fusion.3 = f32[1024]{0:T(1024)S(1)} fusion(s32[4096]{0:T(1024)S(1)} %get-tuple-element.10, f32[4096]{0:T(1024)S(1)} %broadcast.36, f32[]{:T(128)} %constant.14.clone.1), kind=kCustom, calls=%fused_computation.61 | custom fusion | flops 4096 | bytes 4100 | tf_op jit(solution)/shard_map/scatter-add | solution.py:48
  366.1 7.8 %scatter_custom_fusion.5 = f32[1024]{0:T(1024)S(1)} fusion(s32[1024]{0:T(1024)} %param.7, f32[1024]{0:T(1024)S(1)} %add.63, f32[]{:T(128)} %constant.14.clone.1), kind=kCustom, calls=%fused_computation.57 | custom fusion | flops 1024 | bytes 4608 | tf_op jit(solution)/shard_map/scatter-add | solution.py:54
  373.8 1.3 dynamic-slice
  375.7 72.2 %all-reduce = f32[1024]{0:T(1024)S(1)} all-reduce(f32[1024]{0:T(1024)S(1)} %scatter_custom_fusion.5), channel_id=5, replica_groups=mesh['chan'=32,'freq'=16] {'chan'}, use_global_device_ids=true, to_apply=%region_10.11.clone | all-reduce | flops 1024 | bytes 8192
  448.0 11.8 %reduce-scatter.2.cloned.1.call-done = f32[32,256]{1,0:T(8,128)} async-done(((f32[1024,256]{1,0:T(8,128)}), f32[32,256]{1,0:T(8,128)}) %reduce-scatter.2.cloned.1.call-update) | async-done | bytes 32784 | tf_op jit(solution)/shard_map/reduce_scatter | solution.py:56
  459.7 93.2 %psum.7 = f32[32,256]{1,0:T(8,128)S(1)} all-reduce(f32[32,256]{1,0:T(8,128)} %reduce-scatter.2.cloned.1.call-done), channel_id=1, replica_groups=mesh['chan'=32,'freq'=16] {'freq'}, use_global_device_ids=true, to_apply=%region_6.7 | all-reduce | flops 8192 | bytes 65536 | tf_op jit(solution)/shard_map/psum | solution.py:59
  553.0 0.7 broadcast_divide_fusion
  (24 shorter events, 0.6 us)
Async XLA Ops:
  6.5 1.2 copy-start
  6.5 5.1 copy-start.4
  6.5 105.8 %all-gather.7.cloned.1.call-start = ((), (), s32[]{:S(2)}) async-start(), calls=%async_computation.3 | async-start | bytes 16220160 | tf_op jit(solution)/shard_map/all_gather | solution.py:44
  9.6 205.5 %all-gather.5.cloned.1.call-start = ((), (), s32[]{:S(2)}) async-start(), calls=%async_computation.2 | async-start | bytes 16220160 | tf_op jit(solution)/shard_map/all_gather | solution.py:44
  11.5 448.2 %reduce-scatter.2.cloned.1.call-start = ((), (), s32[]{:S(2)}) async-start(), calls=%async_computation.1 | async-start | bytes 1081344 | tf_op jit(solution)/shard_map/reduce_scatter | solution.py:56
  224.0 1.0 copy-start.1
  231.9 0.9 copy-start.3
  231.9 1.2 copy-start.2
Sparse Core Ops, SparseCore 0:
  9.7 102.6 all-gather.6
  114.5 100.4 all-gather.4
  308.4 151.3 reduce-scatter.1
